TPU v7x, 256 devices: a whole 4x4x8 slice. The times are simulated.
256 devices in a mesh: band: 32 (over z, y_lo, core), hid: 8 (over x, y_hi).
Axes of the slice: x: 4, y: 4 (y_hi: 2, y_lo: 2; y = y_hi * 2 + y_lo), z: 8, core: 2. Of those that a mesh axis runs over, the one named last changes fastest.
Arguments:
- pair: float32 [768, 768, 128], P('band', 'hid'), may hold values from -40 to 40
- residue_mask: int32 [768], replicated, may hold values 0 or 1
- hotspot: int32 [768], replicated, may hold values 0 or 1
- interface: int32 [768, 768], P('band', 'hid'), may hold values 0 or 1
- proj_weight: float32 [2, 128, 512], replicated, may hold values from -0.5 to 0.5
- gate_weight: float32 [2, 128, 128], replicated, may hold values from -0.5 to 0.5
- out_weight: float32 [2, 128, 128], replicated, may hold values from -0.5 to 0.5
Outputs:
- pair_out: float32 [768, 768, 128], P('band', 'hid')
All inputs are finite; a program needn't handle non-finite values. No bound on the sum of `interface` on one device may be relied on, other than what follows from the above.
Results may differ from a plain program's by a relative error of at most 0.0021.
Values may be sent and summed in bfloat16 or wider, within the bound.
No kernel may reach another device: no remote copies, remote signals or barrier semaphores. Data moves between devices by JAX's collectives and lax.ppermute only.
A program may use at most 128 MiB of HBM per device.

v0:
```python
import jax
import jax.numpy as jnp
from jax import lax
from jax.sharding import PartitionSpec as P

EPS = 1e-05
HIGH = lax.Precision.HIGHEST


def normalize(values):
    average = jnp.mean(values, axis=-1, keepdims=True)
    centred = values - average
    variance = jnp.mean(centred * centred, axis=-1, keepdims=True)
    return centred * lax.rsqrt(variance + EPS)


def project(state, edge, weight):
    normed = normalize(state)
    proj = jnp.einsum("rmc,cf->frm", normed, weight, precision=HIGH)
    width = weight.shape[1] // 4
    left = (edge * jax.nn.sigmoid(proj[width : 2 * width]) * proj[:width]).astype(jnp.bfloat16)
    right = (edge * jax.nn.sigmoid(proj[3 * width :]) * proj[2 * width : 3 * width]).astype(
        jnp.bfloat16
    )
    return (normed, left, right)


def outgoing(left, right):
    return lax.dot_general(
        left,
        lax.all_gather(right, "band", axis=1, tiled=True),
        (((2,), (2,)), ((0,), (0,))),
        preferred_element_type=jnp.float32,
    )


def incoming(left, right):
    columns = lax.all_to_all(left, "band", split_axis=2, concat_axis=1, tiled=True)
    return lax.dot_general(
        columns,
        lax.all_gather(right, "band", axis=1, tiled=True),
        (((1,), (1,)), ((0,), (0,))),
        preferred_element_type=jnp.float32,
    )


def finish(tri, normed, gate_w, out_w):
    gating = jax.nn.sigmoid(jnp.einsum("rmd,dc->rmc", normed, gate_w, precision=HIGH))
    gathered = lax.all_to_all(tri, "hid", split_axis=2, concat_axis=0, tiled=True)
    average = jnp.mean(gathered, axis=0)
    variance = jnp.mean(gathered * gathered, axis=0) - average * average
    scaled = (gathered - average) * lax.rsqrt(variance + EPS)
    projected = jnp.einsum("hrm,hc->rmc", scaled, out_w, precision=HIGH)
    return gating * projected


def on_device(pair, residue_mask, hotspot, interface, proj_weight, gate_weight, out_weight):
    rows = pair.shape[0]
    cols = pair.shape[1]
    row_start = lax.axis_index("band") * rows
    col_start = lax.axis_index("hid") * cols
    row_mask = lax.dynamic_slice_in_dim(residue_mask, row_start, rows, 0)
    col_mask = lax.dynamic_slice_in_dim(residue_mask, col_start, cols, 0)
    row_hot = lax.dynamic_slice_in_dim(hotspot, row_start, rows, 0)
    col_hot = lax.dynamic_slice_in_dim(hotspot, col_start, cols, 0)
    flags = jnp.maximum(interface, jnp.maximum(row_hot[:, None], col_hot[None, :]))
    edge = (row_mask[:, None] * col_mask[None, :] * flags).astype(jnp.float32)
    state = pair
    for layer in range(2):
        normed, left, right = project(state, edge, proj_weight[layer])
        left, right = (
            lax.all_to_all(left, "hid", split_axis=0, concat_axis=2, tiled=True),
            lax.all_to_all(right, "hid", split_axis=0, concat_axis=2, tiled=True),
        )
        if layer == 0:
            tri = outgoing(left, right)
        else:
            tri = incoming(left, right)
        state = state + finish(tri, normed, gate_weight[layer], out_weight[layer])
    return state


def solution(mesh):
    return jax.shard_map(
        on_device,
        mesh=mesh,
        in_specs=(P("band", "hid", None), P(), P(), P("band", "hid"), P(), P(), P()),
        out_specs=P("band", "hid", None),
        check_vma=False,
    )
```

profile of v0, /device:TPU:96, one launch (start us, length us, event | category | flops | bytes accessed | tf_op | source)
XLA Modules:
  0.0 439.6 jit_solution(17324085471123526692)
XLA Ops:
  6.5 0.9 dynamic_slice.12
  7.4 0.8 dynamic_slice.14
  8.2 0.8 dynamic_slice.13
  8.9 0.8 dynamic_slice.15
  9.7 1.8 reduce_sum.72
  11.5 0.8 multiply_reduce_fusion.1
  12.4 3.9 convolution_bitcast_fusion.1
  16.3 0.1 multiply_convert_fusion
  16.4 0.8 fusion.36
  17.2 0.4 copy.28
  17.6 20.8 %all_to_all.120 = bf16[128,24,96]{2,1,0:T(8,128)(2,1)S(1)} all-to-all(bf16[128,24,96]{2,1,0:T(8,128)(2,1)S(1)} %copy.28), channel_id=1, replica_groups=mesh['band'=32,'hid'=8] {'hid'}, dimensions={0} | all-to-all | bytes 1179648 | tf_op jit(solution)/shard_map/all_to_all | solution.py:73
  38.4 0.5 copy.29
  38.9 1.5 all_to_all.94
  40.4 0.4 copy.26
  40.8 16.0 %all_to_all.121 = bf16[128,24,96]{2,1,0:T(8,128)(2,1)S(1)} all-to-all(bf16[128,24,96]{2,1,0:T(8,128)(2,1)S(1)} %copy.26), channel_id=1, replica_groups=mesh['band'=32,'hid'=8] {'hid'}, dimensions={0} | all-to-all | bytes 1179648 | tf_op jit(solution)/shard_map/all_to_all | solution.py:72
  56.9 0.5 copy.27
  57.4 0.6 all_to_all.90
  58.0 92.1 %all-gather.3.cloned.1.call-done = bf16[16,768,768]{2,1,0:T(8,128)(2,1)} async-done(((bf16[16,24,768]{2,1,0:T(8,128)(2,1)}), bf16[16,768,768]{2,1,0:T(8,128)(2,1)}) %all-gather.3.cloned.1.call-update) | async-done | bytes 18874384 | tf_op jit(solution)/shard_map/all_gather | solution.py:31
  150.1 8.9 %fusion.75 = f32[16,24,768]{2,1,0:T(8,128)S(1)} fusion(bf16[16,24,768]{2,1,0:T(8,128)(2,1)S(1)} %all_to_all.90, bf16[16,768,768]{2,1,0:T(8,128)(2,1)} %all-gather.3.cloned.1.call-done), kind=kOutput, calls=%fused_computation.96 | convolution fusion | flops 452984832 | bytes 20643840 | tf_op jit(solution)/shard_map/dot_general | solution.py:29
  159.0 5.0 %copy.30 = f32[16,24,768]{1,0,2:T(8,128)} copy(f32[16,24,768]{2,1,0:T(8,128)S(1)} %fusion.75) | data formatting | bytes 2359296 | tf_op jit(solution)/shard_map/dot_general | solution.py:29
  164.0 7.4 %reshape.61 = f32[8,1,36864]{2,1,0:T(1,128)} reshape(f32[768,16,24]{2,1,0:T(8,128)} %bitcast.87) | data formatting | bytes 2359296
  171.4 6.8 %all-to-all-start.2 = ((f32[8,1,36864]{2,1,0:T(1,128)}), f32[8,1,36864]{2,1,0:T(1,128)S(1)}, u32[]{:S(2)}, u32[]{:S(2)}) async-start(f32[8,1,36864]{2,1,0:T(1,128)} %reshape.61), calls=%async_computation.2 | async-start | bytes 2359296 | tf_op jit(solution)/shard_map/all_to_all | solution.py:49
  178.2 0.0 all-gather.5.cloned.1.call-start
  178.3 2.5 fusion.23
  180.7 16.1 %all-to-all-done.2 = f32[8,1,36864]{2,1,0:T(1,128)S(1)} async-done(((f32[8,1,36864]{2,1,0:T(1,128)}), f32[8,1,36864]{2,1,0:T(1,128)S(1)}, u32[]{:S(2)}, u32[]{:S(2)}) %all-to-all-start.2) | async-done | bytes 1179680 | tf_op jit(solution)/shard_map/all_to_all | solution.py:49
  196.9 0.5 broadcast.117
  197.4 3.4 reduce.4
  200.9 7.2 %reshape.62 = f32[768,16,24]{2,1,0:T(8,128)} reshape(f32[8,36864]{1,0:T(8,128)S(1)} %reduce.4) | data formatting | bytes 2359296
  208.0 5.8 %copy.31 = f32[16,24,8,96]{3,1,0,2:T(8,128)} copy(f32[16,24,8,96]{1,0,3,2:T(8,128)} %bitcast.89) | data formatting | bytes 2359296 | tf_op jit(solution)/shard_map/all_to_all | solution.py:49
  213.9 1.8 bitcast_reduce_fusion.1
  215.7 0.0 copy-done.1
  215.7 0.1 fusion.2
  215.9 1.1 copy-done.3
  217.0 2.9 fusion.74
  220.0 0.8 multiply_reduce_fusion
  220.8 0.2 copy-done.5
  221.0 3.9 convolution_bitcast_fusion
  225.0 0.8 fusion.26
  225.8 0.4 copy.38
  226.2 16.9 %all_to_all.122 = bf16[128,24,96]{2,1,0:T(8,128)(2,1)S(1)} all-to-all(bf16[128,24,96]{2,1,0:T(8,128)(2,1)S(1)} %copy.38), channel_id=1, replica_groups=mesh['band'=32,'hid'=8] {'hid'}, dimensions={0} | all-to-all | bytes 1179648 | tf_op jit(solution)/shard_map/all_to_all | solution.py:73
  243.1 0.5 copy.39
  243.6 1.5 all_to_all.109
  245.1 0.4 copy.33
  245.6 16.0 %all_to_all.123 = bf16[128,24,96]{2,1,0:T(8,128)(2,1)S(1)} all-to-all(bf16[128,24,96]{2,1,0:T(8,128)(2,1)S(1)} %copy.33), channel_id=1, replica_groups=mesh['band'=32,'hid'=8] {'hid'}, dimensions={0} | all-to-all | bytes 1179648 | tf_op jit(solution)/shard_map/all_to_all | solution.py:72
  261.6 3.8 copy.43
  265.4 5.8 %reshape.63 = bf16[32,2,4608]{2,1,0:T(2,128)(2,1)S(1)} reshape(bf16[768,16,24]{2,1,0:T(8,128)(2,1)} %bitcast.92) | data formatting | bytes 1179648
  271.2 29.5 %all_to_all.124 = bf16[32,2,4608]{2,1,0:T(2,128)(2,1)S(1)} all-to-all(bf16[32,2,4608]{2,1,0:T(2,128)(2,1)S(1)} %reshape.63), channel_id=1, replica_groups=mesh['band'=32,'hid'=8] {'band'}, dimensions={0} | all-to-all | bytes 1179648 | tf_op jit(solution)/shard_map/all_to_all | solution.py:38
  300.6 5.7 %reshape.64 = bf16[768,16,24]{2,1,0:T(8,128)(2,1)} reshape(bf16[32,2,4608]{2,1,0:T(2,128)(2,1)S(1)} %all_to_all.124) | data formatting | bytes 1179648
  306.3 5.7 %copy.37 = bf16[16,32,24,24]{2,1,3,0:T(8,128)(2,1)} copy(bf16[16,32,24,24]{2,0,3,1:T(8,128)(2,1)} %bitcast.91) | data formatting | bytes 1179648 | tf_op jit(solution)/shard_map/all_to_all | solution.py:38
  312.0 5.3 %all_to_all.105 = bf16[16,768,24]{1,2,0:T(8,128)(2,1)S(1)} reshape(bf16[16,32,24,24]{2,1,3,0:T(8,128)(2,1)} %copy.37) | data formatting | bytes 1179648 | tf_op jit(solution)/shard_map/all_to_all | solution.py:38
  317.3 48.6 %all-gather.5.cloned.1.call-done = bf16[16,768,768]{2,1,0:T(8,128)(2,1)} async-done(((bf16[16,24,768]{2,1,0:T(8,128)(2,1)}), bf16[16,768,768]{2,1,0:T(8,128)(2,1)}) %all-gather.5.cloned.1.call-update) | async-done | bytes 18874384 | tf_op jit(solution)/shard_map/all_gather | solution.py:41
  365.9 7.7 %fusion.76 = f32[16,24,768]{2,1,0:T(8,128)S(1)} fusion(bf16[16,768,24]{1,2,0:T(8,128)(2,1)S(1)} %all_to_all.105, bf16[16,768,768]{2,1,0:T(8,128)(2,1)} %all-gather.5.cloned.1.call-done), kind=kOutput, calls=%fused_computation.97 | convolution fusion | flops 452984832 | bytes 20643840 | tf_op jit(solution)/shard_map/dot_general | solution.py:39
  373.6 5.0 %copy.40 = f32[16,24,768]{1,0,2:T(8,128)} copy(f32[16,24,768]{2,1,0:T(8,128)S(1)} %fusion.76) | data formatting | bytes 2359296 | tf_op jit(solution)/shard_map/dot_general | solution.py:39
  378.6 7.4 %reshape.65 = f32[8,1,36864]{2,1,0:T(1,128)} reshape(f32[768,16,24]{2,1,0:T(8,128)} %bitcast.88) | data formatting | bytes 2359296
  386.0 7.0 %all-to-all-start.6 = ((f32[8,1,36864]{2,1,0:T(1,128)}), f32[8,1,36864]{2,1,0:T(1,128)S(1)}, u32[]{:S(2)}, u32[]{:S(2)}) async-start(f32[8,1,36864]{2,1,0:T(1,128)} %reshape.65), calls=%async_computation.6 | async-start | bytes 2359296 | tf_op jit(solution)/shard_map/all_to_all | solution.py:49
  393.0 2.5 fusion.25
  395.5 16.1 %all-to-all-done.6 = f32[8,1,36864]{2,1,0:T(1,128)S(1)} async-done(((f32[8,1,36864]{2,1,0:T(1,128)}), f32[8,1,36864]{2,1,0:T(1,128)S(1)}, u32[]{:S(2)}, u32[]{:S(2)}) %all-to-all-start.6) | async-done | bytes 1179680 | tf_op jit(solution)/shard_map/all_to_all | solution.py:49
  411.7 3.4 reduce.5
  415.1 7.2 %reshape.66 = f32[768,16,24]{2,1,0:T(8,128)} reshape(f32[8,36864]{1,0:T(8,128)S(1)} %reduce.5) | data formatting | bytes 2359296
  422.3 5.0 %copy.41 = f32[16,24,8,96]{3,1,0,2:T(8,128)S(1)} copy(f32[16,24,8,96]{1,0,3,2:T(8,128)} %bitcast.90) | data formatting | bytes 2359296 | tf_op jit(solution)/shard_map/all_to_all | solution.py:49
  427.3 0.3 bitcast_reduce_fusion
  427.6 0.1 fusion
  427.8 1.1 copy-done.2
  428.9 3.7 fusion.17
  (39 shorter events, 0.1 us)
Async XLA Ops:
  6.5 5.0 %copy-start = (f32[24,96,128]{2,1,0:T(8,128)S(1)}, f32[24,96,128]{2,1,0:T(8,128)}, u32[]{:S(2)}) copy-start(f32[24,96,128]{2,1,0:T(8,128)} %param.7) | copy-start | bytes 3538948
  6.5 143.6 %all-gather.3.cloned.1.call-start = ((), (), s32[]{:S(2)}) async-start(), calls=%async_computation.7 | async-start | bytes 19464192 | tf_op jit(solution)/shard_map/all_gather | solution.py:31
  9.7 2.7 copy-start.4
  12.3 4.0 copy-start.12
  12.3 4.0 copy-start.14
  16.4 0.8 copy-start.8
  171.4 6.9 %copy-start.13 = (f32[24,96]{1,0:T(8,128)S(1)}, f32[24,96]{1,0:T(8,128)}, u32[]{:S(2)}) copy-start(f32[24,96]{1,0:T(8,128)} %copy-done.12) | copy-start | bytes 27652
  171.4 6.9 %copy-start.15 = (f32[2,128,128]{2,1,0:T(8,128)S(1)}, f32[2,128,128]{2,1,0:T(8,128)}, u32[]{:S(2)}) copy-start(f32[2,128,128]{2,1,0:T(8,128)} %param.12) | copy-start | bytes 393220
  171.4 25.5 %all-to-all-start.2 = ((f32[8,1,36864]{2,1,0:T(1,128)}), f32[8,1,36864]{2,1,0:T(1,128)S(1)}, u32[]{:S(2)}, u32[]{:S(2)}) async-start(f32[8,1,36864]{2,1,0:T(1,128)} %reshape.61), calls=%async_computation.2 | async-start | bytes 2359296 | tf_op jit(solution)/shard_map/all_to_all | solution.py:49
  178.2 187.7 %all-gather.5.cloned.1.call-start = ((), (), s32[]{:S(2)}) async-start(), calls=%async_computation.8 | async-start | bytes 19464192 | tf_op jit(solution)/shard_map/all_gather | solution.py:41
  213.9 1.9 copy-start.1
  215.7 1.3 copy-start.3
  215.7 1.3 copy-start.6
  220.0 1.0 copy-start.5
  221.0 3.9 copy-start.10
  221.0 3.9 copy-start.9
  386.0 7.1 %copy-start.11 = (f32[24,96]{1,0:T(8,128)S(1)}, f32[24,96]{1,0:T(8,128)}, u32[]{:S(2)}) copy-start(f32[24,96]{1,0:T(8,128)} %copy-done.10) | copy-start | bytes 27652
  386.0 7.1 %copy-start.16 = (f32[2,128,128]{2,1,0:T(8,128)S(1)}, f32[2,128,128]{2,1,0:T(8,128)}, u32[]{:S(2)}) copy-start(f32[2,128,128]{2,1,0:T(8,128)} %param.12) | copy-start | bytes 393220
  386.0 25.7 %all-to-all-start.6 = ((f32[8,1,36864]{2,1,0:T(1,128)}), f32[8,1,36864]{2,1,0:T(1,128)S(1)}, u32[]{:S(2)}, u32[]{:S(2)}) async-start(f32[8,1,36864]{2,1,0:T(1,128)} %reshape.65), calls=%async_computation.6 | async-start | bytes 2359296 | tf_op jit(solution)/shard_map/all_to_all | solution.py:49
  427.6 1.3 copy-start.2
  427.6 1.3 copy-start.7
Sparse Core Ops, SparseCore 0:
  40.5 109.5 all-gather.2
  245.2 120.5 all-gather.4
where the time goes:
time: 446 us; the launch traced here: 440 us
  waiting for transfers between devices  173 us (39%)
  blocking collectives  99.2 us (22%)
  local copies, waits for them, and re-layouts  89 us (20%)
  matrix products  36.1 us (8%)
  other arithmetic  14.4 us (3%)
  starting transfers between devices  13.9 us (3%)
  between operations  13.9 us (3%)
    all_gather x1, waiting for transfers between devices, outgoing(): lax.all_gather(right, 'band', axis=1, tiled=True)  92.1 us
    all_gather x1, waiting for transfers between devices, incoming(): lax.all_gather(right, 'band', axis=1, tiled=True)  48.6 us
    unnamed x40, local copies, waits for them, and re-layouts  43 us
    all_to_all x2, blocking collectives, on_device(): lax.all_to_all(right, 'hid', split_axis=0, concat_axis=2, tiled=True)  37.7 us
    all_to_all x2, waiting for transfers between devices, finish(): lax.all_to_all(tri, 'hid', split_axis=2, concat_axis=0, tiled=True)  32.3 us
    all_to_all x2, blocking collectives, on_device(): lax.all_to_all(left, 'hid', split_axis=0, concat_axis=2, tiled=True)  32 us
    all_to_all x1, blocking collectives, incoming(): lax.all_to_all(left, 'band', split_axis=2, concat_axis=1, tiled=True)  29.5 us
    all_to_all x2, starting transfers between devices, finish(): lax.all_to_all(tri, 'hid', split_axis=2, concat_axis=0, tiled=True)  13.9 us
  transfers between devices with their start and end apart: 4, of which 4 were waited for; matrix products, arithmetic and copies ran while one was open for 6% of the time, Pallas kernels for 0%

commit v1 on v0

--- a/solution.py
+++ b/solution.py
@@ -38,7 +38,9 @@
     columns = lax.all_to_all(left, "band", split_axis=2, concat_axis=1, tiled=True)
     return lax.dot_general(
         columns,
-        lax.all_gather(right, "band", axis=1, tiled=True),
+        jnp.concatenate(
+            lax.all_to_all(jnp.stack([right] * lax.axis_size("band")), "band", 0, 0), axis=1
+        ),
         (((1,), (1,)), ((0,), (0,))),
         preferred_element_type=jnp.float32,
     )

time: 446 us -> 793 us (1.78)
  the two profiles are of different devices: /device:TPU:96 before, /device:TPU:1 now
where the time goes in v1:
time: 793 us; the launch traced here: 786 us
  waiting for transfers between devices  551 us (69%)
  local copies, waits for them, and re-layouts  107 us (13%)
  blocking collectives  34.7 us (4%)
  starting transfers between devices  33.4 us (4%)
  matrix products  30.9 us (4%)
  other arithmetic  14.3 us (2%)
  between operations  14 us (2%)
    all_to_all x1, waiting for transfers between devices, incoming(): lax.all_to_all(jnp.stack([right] * lax.axis_size('band')), 'band', 0, 0)  394 us
    all_gather x1, waiting for transfers between devices, outgoing(): lax.all_gather(right, 'band', axis=1, tiled=True)  95.7 us
    unnamed x40, local copies, waits for them, and re-layouts  43.6 us
    all_to_all x2, waiting for transfers between devices, finish(): lax.all_to_all(tri, 'hid', split_axis=2, concat_axis=0, tiled=True)  30.4 us
    all_to_all x1, blocking collectives, on_device(): lax.all_to_all(right, 'hid', split_axis=0, concat_axis=2, tiled=True)  19.8 us
    all_to_all x1, waiting for transfers between devices, incoming(): lax.all_to_all(left, 'band', split_axis=2, concat_axis=1, tiled=True)  17 us
  transfers between devices with their start and end apart: 7, of which 7 were waited for; matrix products, arithmetic and copies ran while one was open for 4% of the time, Pallas kernels for 0%

profile of v1, /device:TPU:1, one launch (start us, length us, event | category | flops | bytes accessed | tf_op | source)
XLA Modules:
  0.0 785.5 jit_solution(8897681517351206196)
XLA Ops:
  6.5 0.9 dynamic_slice.12
  7.4 0.8 dynamic_slice.14
  8.2 0.8 dynamic_slice.13
  8.9 0.8 dynamic_slice.15
  9.7 1.8 reduce_sum.72
  11.5 0.8 multiply_reduce_fusion.1
  12.4 3.9 convolution_bitcast_fusion.1
  16.4 0.8 fusion.36
  17.2 0.4 copy.27
  17.6 19.8 %all_to_all.122 = bf16[128,24,96]{2,1,0:T(8,128)(2,1)S(1)} all-to-all(bf16[128,24,96]{2,1,0:T(8,128)(2,1)S(1)} %copy.27), channel_id=1, replica_groups=mesh['band'=32,'hid'=8] {'hid'}, dimensions={0} | all-to-all | bytes 1179648 | tf_op jit(solution)/shard_map/all_to_all | solution.py:75
  37.5 0.5 copy.28
  38.0 1.5 all_to_all.95
  39.5 0.4 copy.25
  39.9 14.8 %all_to_all.123 = bf16[128,24,96]{2,1,0:T(8,128)(2,1)S(1)} all-to-all(bf16[128,24,96]{2,1,0:T(8,128)(2,1)S(1)} %copy.25), channel_id=1, replica_groups=mesh['band'=32,'hid'=8] {'hid'}, dimensions={0} | all-to-all | bytes 1179648 | tf_op jit(solution)/shard_map/all_to_all | solution.py:74
  54.7 0.5 copy.26
  55.2 0.6 all_to_all.91
  55.9 95.7 %all-gather.2.cloned.1.call-done = bf16[16,768,768]{2,1,0:T(8,128)(2,1)} async-done(((bf16[16,24,768]{2,1,0:T(8,128)(2,1)}), bf16[16,768,768]{2,1,0:T(8,128)(2,1)}) %all-gather.2.cloned.1.call-update) | async-done | bytes 18874384 | tf_op jit(solution)/shard_map/all_gather | solution.py:31
  151.6 8.9 %fusion.75 = f32[16,24,768]{2,1,0:T(8,128)S(1)} fusion(bf16[16,24,768]{2,1,0:T(8,128)(2,1)S(1)} %all_to_all.91, bf16[16,768,768]{2,1,0:T(8,128)(2,1)} %all-gather.2.cloned.1.call-done), kind=kOutput, calls=%fused_computation.96 | convolution fusion | flops 452984832 | bytes 20643840 | tf_op jit(solution)/shard_map/dot_general | solution.py:29
  160.5 5.0 copy.29
  165.5 7.3 reshape.72
  172.8 6.2 all-to-all-start.2
  179.0 2.5 fusion.23
  181.5 15.4 %all-to-all-done.2 = f32[8,1,36864]{2,1,0:T(1,128)S(1)} async-done(((f32[8,1,36864]{2,1,0:T(1,128)}), f32[8,1,36864]{2,1,0:T(1,128)S(1)}, u32[]{:S(2)}, u32[]{:S(2)}) %all-to-all-start.2) | async-done | bytes 1179680 | tf_op jit(solution)/shard_map/all_to_all | solution.py:51
  196.9 0.5 broadcast.118
  197.4 3.4 reduce.4
  200.7 7.2 reshape.73
  207.9 6.0 copy.30
  214.0 1.8 bitcast_reduce_fusion.1
  216.0 1.1 copy-done.3
  217.1 2.9 fusion.74
  220.1 0.8 multiply_reduce_fusion
  221.1 3.9 convolution_bitcast_fusion
  225.1 0.8 fusion.26
  225.9 1.3 copy.32
  227.1 3.5 all-to-all-start.3
  230.7 1.3 copy.37
  232.0 11.4 %all-to-all-done.3 = bf16[128,24,96]{2,1,0:T(8,128)(2,1)S(1)} async-done(((bf16[128,24,96]{2,1,0:T(8,128)(2,1)}), bf16[128,24,96]{2,1,0:T(8,128)(2,1)S(1)}, u32[]{:S(2)}, u32[]{:S(2)}) %all-to-all-start.3) | async-done | bytes 589856 | tf_op jit(solution)/shard_map/all_to_all | solution.py:74
  243.4 3.9 all-to-all-start.5
  247.3 3.8 copy.43
  251.1 6.4 reshape.74
  257.5 2.6 all-to-all-done.5
  260.1 8.8 %all-to-all-start.4 = ((bf16[32,2,4608]{2,1,0:T(2,128)(2,1)}), bf16[32,2,4608]{2,1,0:T(2,128)(2,1)S(1)}, u32[]{:S(2)}, u32[]{:S(2)}) async-start(bf16[32,2,4608]{2,1,0:T(2,128)(2,1)} %reshape.74), calls=%async_computation.4 | async-start | bytes 1179648 | tf_op jit(solution)/shard_map/all_to_all | solution.py:38
  268.9 0.5 copy.38
  269.4 0.6 stack.4
  270.1 17.0 %all-to-all-done.4 = bf16[32,2,4608]{2,1,0:T(2,128)(2,1)S(1)} async-done(((bf16[32,2,4608]{2,1,0:T(2,128)(2,1)}), bf16[32,2,4608]{2,1,0:T(2,128)(2,1)S(1)}, u32[]{:S(2)}, u32[]{:S(2)}) %all-to-all-start.4) | async-done | bytes 589856 | tf_op jit(solution)/shard_map/all_to_all | solution.py:38
  287.0 6.9 stack.5
  293.9 6.3 all-to-all-start.6
  300.2 5.7 reshape.75
  305.9 5.6 copy.36
  311.5 5.3 all_to_all.106
  316.7 394.3 %all-to-all-done.6 = bf16[32,16,24,768]{3,2,1,0:T(8,128)(2,1)} async-done(((bf16[32,16,24,768]{3,2,1,0:T(8,128)(2,1)}), bf16[32,16,24,768]{3,2,1,0:T(8,128)(2,1)}, u32[]{:S(2)}, u32[]{:S(2)}) %all-to-all-start.6) | async-done | bytes 18874400 | tf_op jit(solution)/shard_map/all_to_all | solution.py:42
  711.0 9.5 %copy.39 = bf16[16,32,24,768]{3,2,1,0:T(8,128)(2,1)S(1)} copy(bf16[16,32,24,768]{3,2,0,1:T(8,128)(2,1)} %bitcast.27) | data formatting | bytes 37748736 | tf_op jit(solution)/shard_map/reshape | solution.py:41
  720.5 2.6 fusion.76
  723.1 5.0 copy.40
  728.1 7.3 reshape.76
  735.5 4.6 all-to-all-start.7
  740.1 2.5 fusion.25
  742.6 15.0 %all-to-all-done.7 = f32[8,1,36864]{2,1,0:T(1,128)S(1)} async-done(((f32[8,1,36864]{2,1,0:T(1,128)}), f32[8,1,36864]{2,1,0:T(1,128)S(1)}, u32[]{:S(2)}, u32[]{:S(2)}) %all-to-all-start.7) | async-done | bytes 1179680 | tf_op jit(solution)/shard_map/all_to_all | solution.py:51
  757.6 3.4 reduce.5
  761.0 7.2 reshape.77
  768.2 5.0 copy.41
  773.2 0.3 bitcast_reduce_fusion
  773.7 1.1 copy-done.2
  774.8 3.7 fusion.17
  (43 shorter events, 0.7 us)
Async XLA Ops:
  6.5 5.0 copy-start
  6.5 145.0 %all-gather.2.cloned.1.call-start = ((), (), s32[]{:S(2)}) async-start(), calls=%async_computation.8 | async-start | bytes 19464192 | tf_op jit(solution)/shard_map/all_gather | solution.py:31
  9.7 2.7 copy-start.4
  12.3 4.0 copy-start.12
  12.3 4.0 copy-start.14
  16.4 0.8 copy-start.8
  172.8 6.2 copy-start.13
  172.8 6.2 copy-start.15
  172.8 24.1 %all-to-all-start.2 = ((f32[8,1,36864]{2,1,0:T(1,128)}), f32[8,1,36864]{2,1,0:T(1,128)S(1)}, u32[]{:S(2)}, u32[]{:S(2)}) async-start(f32[8,1,36864]{2,1,0:T(1,128)} %reshape.72), calls=%async_computation.2 | async-start | bytes 2359296 | tf_op jit(solution)/shard_map/all_to_all | solution.py:51
  214.0 1.9 copy-start.1
  215.8 1.3 copy-start.3
  215.8 1.3 copy-start.6
  220.1 1.0 copy-start.5
  221.1 3.9 copy-start.10
  221.1 3.9 copy-start.9
  227.1 16.3 %all-to-all-start.3 = ((bf16[128,24,96]{2,1,0:T(8,128)(2,1)}), bf16[128,24,96]{2,1,0:T(8,128)(2,1)S(1)}, u32[]{:S(2)}, u32[]{:S(2)}) async-start(bf16[128,24,96]{2,1,0:T(8,128)(2,1)} %copy.32), calls=%async_computation.3 | async-start | bytes 1572864 | tf_op jit(solution)/shard_map/all_to_all | solution.py:74
  243.4 16.7 %all-to-all-start.5 = ((bf16[128,24,96]{2,1,0:T(8,128)(2,1)}), bf16[128,24,96]{2,1,0:T(8,128)(2,1)S(1)}, u32[]{:S(2)}, u32[]{:S(2)}) async-start(bf16[128,24,96]{2,1,0:T(8,128)(2,1)} %copy.37), calls=%async_computation.5 | async-start | bytes 1572864 | tf_op jit(solution)/shard_map/all_to_all | solution.py:75
  260.1 27.0 %all-to-all-start.4 = ((bf16[32,2,4608]{2,1,0:T(2,128)(2,1)}), bf16[32,2,4608]{2,1,0:T(2,128)(2,1)S(1)}, u32[]{:S(2)}, u32[]{:S(2)}) async-start(bf16[32,2,4608]{2,1,0:T(2,128)(2,1)} %reshape.74), calls=%async_computation.4 | async-start | bytes 1179648 | tf_op jit(solution)/shard_map/all_to_all | solution.py:38
  293.9 417.1 %all-to-all-start.6 = ((bf16[32,16,24,768]{3,2,1,0:T(8,128)(2,1)}), bf16[32,16,24,768]{3,2,1,0:T(8,128)(2,1)}, u32[]{:S(2)}, u32[]{:S(2)}) async-start(bf16[32,16,24,768]{3,2,1,0:T(8,128)(2,1)} %stack.5), calls=%async_computation.6 | async-start | bytes 37748736 | tf_op jit(solution)/shard_map/all_to_all | solution.py:42
  735.5 4.6 copy-start.11
  735.5 4.7 copy-start.16
  735.5 22.2 %all-to-all-start.7 = ((f32[8,1,36864]{2,1,0:T(1,128)}), f32[8,1,36864]{2,1,0:T(1,128)S(1)}, u32[]{:S(2)}, u32[]{:S(2)}) async-start(f32[8,1,36864]{2,1,0:T(1,128)} %reshape.76), calls=%async_computation.7 | async-start | bytes 2359296 | tf_op jit(solution)/shard_map/all_to_all | solution.py:51
  773.5 1.3 copy-start.2
  773.5 1.3 copy-start.7
Sparse Core Ops, SparseCore 0:
  39.6 111.9 all-gather.1
